TPU v7x, 32 devices: a whole 2x2x4 slice. The times are simulated.
32 devices in a mesh: req: 16 (over z, y, x), tp: 2 (over core).
Axes of the slice: x: 2, y: 2, z: 4, core: 2. Of those that a mesh axis runs over, the one named last changes fastest.
Arguments:
- tokens: bfloat16 [8192, 3072], P('req', 'tp'), may hold values from -6 to 6
- norm_gain: bfloat16 [3072], P('tp'), may hold values from 0.099609375 to 1.8984375
- qkv_weight: bfloat16 [3, 3072, 3072], P(None, 'req', 'tp'), may hold values from -0.109375 to 0.109375
- out_weight: bfloat16 [3072, 3072], P('tp', 'req'), may hold values from -1.75 to 1.75
- cache: bfloat16 [16, 2, 2048, 3072], P('req', None, None, 'tp'), may hold values from -720 to 720
- cache_lens: int32 [16], P('req'), may hold values from 0 to 2048, as said below
- valid_tokens: int32 [16], P('req'), may hold values from 128 to 512, as said below
Outputs:
- mixed: bfloat16 [8192, 3072], P('req', 'tp')
- new_entries: bfloat16 [16, 2, 512, 3072], P('req', None, None, 'tp')
Inputs may be any that keep to these rules, and one draw needn't show every extreme that they name: `cache_lens`: in every draw some request's cache holds all 2048 entries and some request's cache is empty. `valid_tokens`: in every draw some request brings 512 live new tokens.
All inputs are finite; a program needn't handle non-finite values.
Results may differ from a plain program's by a relative error of at most 0.0095.
The roundings to bfloat16 on the way count: a program that leaves them out, or rounds other values in their place, can miss the bound.
Values may be sent and summed in bfloat16 or wider, within the bound.
A program may use at most 192 MiB of HBM per device.

v0:
```python
import math
import jax
import jax.numpy as jnp
from jax import lax
from jax.sharding import PartitionSpec as P

HD = 96
epsilon = 1e-05
masked_value = -1e30
theta_base = 10000.0


def rotate(projected, positions):
    tokens_here, columns = projected.shape
    per_head = projected.reshape(tokens_here, columns // HD, HD)
    frequencies = jnp.power(theta_base, -jnp.arange(0, HD, 2, dtype=jnp.float32) / HD)
    angles = positions.astype(jnp.float32)[:, None] * frequencies[None, :]
    cosine = jnp.cos(angles)[:, None, :]
    sine_table = jnp.sin(angles)[:, None, :]
    first_half = per_head[..., : HD // 2]
    second_half = per_head[..., HD // 2 :]
    turned = jnp.concatenate(
        [
            first_half * cosine - second_half * sine_table,
            second_half * cosine + first_half * sine_table,
        ],
        axis=-1,
    )
    return turned.reshape(tokens_here, columns)


def add_rows(source, piece):
    return jnp.einsum("td,jdc->jtc", source, piece, preferred_element_type=jnp.float32)


def score_block(queries, key_rows, score_scale):
    return (
        lax.dot_general(
            queries, key_rows, (((1,), (1,)), ((), ())), preferred_element_type=jnp.float32
        )
        * score_scale
    )


def attend_whole(
    queries, cache_keys, cache_values, keys_new, values_new, length, live_mask, score_scale
):
    cache_scores = score_block(queries, cache_keys, score_scale)
    cache_ids = jnp.arange(cache_keys.shape[0], dtype=jnp.int32)
    cache_scores = jnp.where((cache_ids < length)[None, :], cache_scores, masked_value)
    new_scores = jnp.where(live_mask, score_block(queries, keys_new, score_scale), masked_value)
    scores = jnp.concatenate([cache_scores, new_scores], axis=1)
    maximum = jnp.max(scores, axis=1, keepdims=True)
    expo = jnp.exp(scores - maximum)
    weights = (expo / jnp.sum(expo, axis=1, keepdims=True)).astype(jnp.bfloat16)
    value_rows = jnp.concatenate([cache_values, values_new], axis=0)
    return jnp.dot(weights, value_rows, preferred_element_type=jnp.float32).astype(jnp.bfloat16)


def attend_all(
    queries, keys_new, values_new, cache_keys, cache_values, length, live_mask, score_scale
):
    query_rows, head_cols = queries.shape

    def per_head(head_index):
        col_start = head_index * HD

        def select(source):
            return lax.dynamic_slice_in_dim(source, col_start, HD, 1)

        return attend_whole(
            select(queries),
            select(cache_keys),
            select(cache_values),
            select(keys_new),
            select(values_new),
            length,
            live_mask,
            score_scale,
        )

    heads_out = lax.map(per_head, jnp.arange(head_cols // HD, dtype=jnp.int32))
    return jnp.transpose(heads_out, (1, 0, 2)).reshape(query_rows, head_cols)


def per_device(tokens, norm_gain, qkv_weight, out_weight, cache, cache_lens, valid_tokens):
    gathered, gain_all = (
        lax.all_gather(tokens, "tp", axis=1, tiled=True),
        lax.all_gather(norm_gain, "tp", axis=0, tiled=True),
    )
    inputs = gathered.astype(jnp.float32)
    spread = jnp.mean(inputs * inputs, axis=-1, keepdims=True)
    normed = (inputs * lax.rsqrt(spread + epsilon) * gain_all.astype(jnp.float32)).astype(
        jnp.bfloat16
    )
    new_rows = normed.shape[0]
    length = cache_lens[0]
    valid_count = valid_tokens[0]
    token_ids = jnp.arange(new_rows, dtype=jnp.int32)
    positions = length + token_ids
    projected = add_rows(normed, lax.all_gather(qkv_weight, "req", axis=1, tiled=True))
    combined = jnp.stack(
        [rotate(projected[0], positions), rotate(projected[1], positions), projected[2]]
    ).astype(jnp.bfloat16)
    queries = combined[0]
    keys_new = combined[1]
    values_new = combined[2]
    kept = (token_ids < valid_count)[:, None]
    new_entries = jnp.stack(
        [
            jnp.where(kept, keys_new, jnp.zeros_like(keys_new)),
            jnp.where(kept, values_new, jnp.zeros_like(values_new)),
        ]
    )[None]
    live_mask = (token_ids[None, :] <= token_ids[:, None]) & (token_ids[None, :] < valid_count)
    cache_keys = cache[0, 0]
    cache_values = cache[0, 1]
    score_scale = 1.0 / math.sqrt(HD)
    attended = attend_all(
        queries, keys_new, values_new, cache_keys, cache_values, length, live_mask, score_scale
    )
    partial_value = jnp.dot(
        attended,
        lax.all_gather(out_weight, "req", axis=1, tiled=True),
        preferred_element_type=jnp.float32,
    )
    summed = lax.psum_scatter(
        partial_value.astype(jnp.bfloat16), "tp", scatter_dimension=1, tiled=True
    ).astype(jnp.float32)
    mixed_out = jnp.where(kept, summed, jnp.zeros_like(summed)).astype(jnp.bfloat16)
    return (mixed_out, new_entries)


def solution(mesh):
    placed = (
        P("req", "tp"),
        P("tp"),
        P(None, "req", "tp"),
        P("tp", "req"),
        P("req", None, None, "tp"),
        P("req"),
        P("req"),
    )
    return jax.shard_map(
        per_device,
        mesh=mesh,
        in_specs=placed,
        out_specs=(P("req", "tp"), P("req", None, None, "tp")),
        check_vma=False,
    )
```

profile of v0, /device:TPU:0, one launch (start us, length us, event | category | flops | bytes accessed | tf_op | source)
XLA Modules:
  0.0 568.6 jit_solution(8117036062014066321)
XLA Ops:
  9.5 1.9 all-gather
  12.8 10.4 %slice_bitcast_fusion = (bf16[2048,1536]{1,0:T(8,128)(2,1)}, bf16[2048,1536]{1,0:T(8,128)(2,1)}) fusion(bf16[1,2,2048,1536]{3,2,1,0:T(8,128)(2,1)} %param.13), kind=kLoop, calls=%fused_computation.33 | loop fusion | bytes 25165824 | tf_op jit(solution)/shard_map/squeeze | solution.py:117
  24.4 2.7 fusion.21
  27.1 302.5 %all-gather.7.cloned.1.call-done = bf16[3,3072,1536]{2,1,0:T(8,128)(2,1)} async-done(((bf16[3,192,1536]{2,1,0:T(8,128)(2,1)}), bf16[3,3072,1536]{2,1,0:T(8,128)(2,1)}) %all-gather.7.cloned.1.call-update) | async-done | bytes 28311568 | tf_op jit(solution)/shard_map/all_gather | solution.py:101
  329.6 19.0 %convolution_bitcast_fusion = f32[3,512,1536]{2,1,0:T(8,128)S(1)} fusion(bf16[3,3072,1536]{2,1,0:T(8,128)(2,1)} %all-gather.7.cloned.1.call-done, bf16[512,3072]{1,0:T(8,128)(2,1)S(1)} %copy-done.3, f32[3072]{0:T(1024)S(1)} %bitcast.43, f32[512]{0:T(512)S(1)} %add_rsqrt_fusion), kind=kOutput, calls=%fused_computation.35 | convolution fusion | flops 14501806080 | bytes 40908800 | tf_op jit(solution)/shard_map/td,jdc->jtc/dot_general | solution.py:33
  348.6 3.4 fusion.31
  352.1 2.1 copy-done
  354.1 2.4 copy.17
  356.5 3.5 copy.18
  360.0 3.4 subtract_convert_fusion
  365.5 4.4 broadcast_select_fusion
  369.9 170.7 %while.11 = (s32[]{:T(128)}, bf16[16,512,96]{1,2,0:T(8,128)(2,1)}, s32[]{:T(128)}, s32[16]{0:T(128)S(1)}, bf16[512,1536]{0,1:T(8,128)(2,1)}, /*index=5*/bf16[204...) while((s32[]{:T(128)}, bf16[16,512,96]{1,2,0:T(8,128)(2,1)}, ...), condition=%wide.region_5.6_spmd.clone, body=%wide.region_1.5_spmd.clone.sunk | while | flops 517981184 | bytes 18146508 | solution.py:82
  371.7 2.3 fusion.42
  376.2 1.4 constant_dynamic-slice_fusion.5
  378.7 2.0 fusion.44
  382.4 2.3 fusion.42
  386.8 1.4 constant_dynamic-slice_fusion.5
  389.4 2.0 fusion.44
  393.1 2.3 fusion.42
  397.5 1.5 constant_dynamic-slice_fusion.5
  400.1 2.0 fusion.44
  403.8 2.3 fusion.42
  408.3 1.5 constant_dynamic-slice_fusion.5
  410.8 2.0 fusion.44
  414.5 2.3 fusion.42
  419.0 1.4 constant_dynamic-slice_fusion.5
  421.5 2.0 fusion.44
  425.2 2.3 fusion.42
  429.7 1.4 constant_dynamic-slice_fusion.5
  432.2 2.0 fusion.44
  435.9 2.3 fusion.42
  440.4 1.4 constant_dynamic-slice_fusion.5
  442.9 2.0 fusion.44
  446.6 2.3 fusion.42
  451.0 1.4 constant_dynamic-slice_fusion.5
  453.6 2.0 fusion.44
  457.3 2.3 fusion.42
  461.7 1.4 constant_dynamic-slice_fusion.5
  464.2 2.0 fusion.44
  468.0 2.3 fusion.42
  472.4 1.4 constant_dynamic-slice_fusion.5
  474.9 2.0 fusion.44
  478.7 2.3 fusion.42
  483.1 1.4 constant_dynamic-slice_fusion.5
  485.6 2.0 fusion.44
  489.3 2.3 fusion.42
  493.8 1.4 constant_dynamic-slice_fusion.5
  496.3 2.0 fusion.44
  500.0 2.3 fusion.42
  504.5 1.4 constant_dynamic-slice_fusion.5
  507.0 2.0 fusion.44
  510.7 2.3 fusion.42
  515.2 1.4 constant_dynamic-slice_fusion.5
  517.7 2.0 fusion.44
  521.4 2.3 fusion.42
  525.8 1.4 constant_dynamic-slice_fusion.5
  528.4 2.0 fusion.44
  532.1 2.1 fusion.42
  538.6 2.0 fusion.44
  540.6 9.4 %convolution_convert_fusion = bf16[512,3072]{1,0:T(8,128)(2,1)} fusion(bf16[512,1536]{0,1:T(8,128)(2,1)} %bitcast.44, bf16[1536,3072]{0,1:T(8,128)(2,1)} %all-gather.9.cloned.1.call-done), kind=kOutput, calls=%fused_computation.36 | convolution fusion | flops 4833411072 | bytes 14155776 | tf_op jit(solution)/shard_map/dot_general | solution.py:122
  550.1 1.4 copy-done.1
  551.9 1.9 maximum_bitcast_fusion
  553.9 5.3 reduce-scatter.2.cloned.1.call-done
  559.2 2.9 select_convert_fusion
  (126 shorter events, 78.1 us)
Async XLA Ops:
  7.2 2.3 copy-start.4
  7.2 17.2 %all-gather.5.cloned.1.call-start = ((), (), s32[]{:S(2)}) async-start(), calls=%async_computation.1 | async-start | bytes 4718592 | tf_op jit(solution)/shard_map/all_gather | solution.py:88
  7.9 321.7 %all-gather.7.cloned.1.call-start = ((), (), s32[]{:S(2)}) async-start(), calls=%async_computation.2 | async-start | bytes 30081024 | tf_op jit(solution)/shard_map/all_gather | solution.py:101
  8.7 532.0 %all-gather.9.cloned.1.call-start = ((), (), s32[]{:S(2)}) async-start(), calls=%async_computation.3 | async-start | bytes 10027008 | tf_op jit(solution)/shard_map/all_gather | solution.py:124
  9.4 549.8 %reduce-scatter.2.cloned.1.call-start = ((), (), s32[]{:S(2)}) async-start(), calls=%async_computation.4 | async-start | bytes 4718592 | tf_op jit(solution)/shard_map/reduce_scatter | solution.py:127
  24.4 305.2 %copy-start.3 = (bf16[512,3072]{1,0:T(8,128)(2,1)S(1)}, bf16[512,3072]{1,0:T(8,128)(2,1)}, u32[]{:S(2)}) copy-start(bf16[512,3072]{1,0:T(8,128)(2,1)} %all-gather.5.cloned.1.call-done) | copy-start | bytes 9437188
  348.6 5.5 copy-start
  550.0 1.4 copy-start.1
  550.0 1.9 copy-start.2
Sparse Core Ops, SparseCore 0:
  9.5 14.8 all-gather.4
  27.1 302.4 all-gather.6
  332.4 120.6 all-gather.8
  550.2 8.9 reduce-scatter.1
where the time goes:
time: 571 us; the launch traced here: 569 us
  waiting for transfers between devices  311 us (54%)
  matrix products  117 us (20%)
  local copies, waits for them, and re-layouts  73.2 us (13%)
  other arithmetic  41.3 us (7%)
  between operations  15.2 us (3%)
  loops' own time  9.17 us (2%)
    all_gather x1, waiting for transfers between devices, per_device(): lax.all_gather(qkv_weight, 'req', axis=1, tiled=True)  302 us
    dot_general x32, matrix products, score_block(): lax.dot_general(queries, key_rows, (((1,), (1,)), ((), ())), preferred_el...  57.1 us
    dynamic_slice x32, local copies, waits for them, and re-layouts, select(): return lax.dynamic_slice_in_dim(source, col_start, HD, 1)  40 us
    dot_general x16, matrix products, attend_whole(): jnp.dot(weights, value_rows, preferred_element_type=jnp.float32)  31.4 us
    dot_general x1, matrix products, add_rows(): jnp.einsum('td,jdc->jtc', source, piece, preferred_element_type=jnp.float32)  19 us
    reduce_sum x16, other arithmetic, attend_whole(): weights = (expo / jnp.sum(expo, axis=1, keepdims=True)).astype(jnp.bfloat16)  13.6 us
  transfers between devices with their start and end apart: 4, of which 3 were waited for; matrix products, arithmetic and copies ran while one was open for 38% of the time, Pallas kernels for 0%

commit v1 on v0

--- a/solution.py
+++ b/solution.py
@@ -8,6 +8,23 @@
 epsilon = 1e-05
 masked_value = -1e30
 theta_base = 10000.0
+
+
+def in_order(pieces, dim):
+    shape = list(pieces.shape[1:])
+    shape[dim] *= pieces.shape[0]
+    return jnp.moveaxis(pieces, 0, dim).reshape(shape)
+
+
+def ring_gather(x, axis, dim):
+    peers = lax.axis_size(axis)
+    upward = [(i, (i + 1) % peers) for i in range(peers)]
+    pieces = [x]
+    while len(pieces) < peers:
+        pieces.append(lax.ppermute(pieces[-1], axis, upward))
+    mine = lax.axis_index(axis)
+    pieces = jnp.stack(pieces)[(mine - jnp.arange(peers)) % peers]
+    return in_order(pieces, dim)
 
 
 def rotate(projected, positions):
@@ -98,7 +115,7 @@
     valid_count = valid_tokens[0]
     token_ids = jnp.arange(new_rows, dtype=jnp.int32)
     positions = length + token_ids
-    projected = add_rows(normed, lax.all_gather(qkv_weight, "req", axis=1, tiled=True))
+    projected = add_rows(normed, ring_gather(qkv_weight, "req", 1))
     combined = jnp.stack(
         [rotate(projected[0], positions), rotate(projected[1], positions), projected[2]]
     ).astype(jnp.bfloat16)

time: 571 us -> 1030 us (1.80)
  waiting for transfers between devices: 311 us -> 634 us
  local copies, waits for them, and re-layouts: 73.2 us -> 169 us
  matrix products: 117 us -> 151 us
    ppermute x0 -> x15, waiting for transfers between devices: none -> 632 us  [ring_gather(): pieces.append(lax.ppermute(pieces[-1], axis, upward))]
    all_gather x1 -> x0, waiting for transfers between devices: 302 us -> none  [per_device(): lax.all_gather(qkv_weight, 'req', axis=1, tiled=True)]
    dot_general x16, matrix products: 31.4 us -> 65 us  [attend_whole(): jnp.dot(weights, value_rows, preferred_element_type=jnp.float32)]
    unnamed x11 -> x49, local copies, waits for them, and re-layouts: 3.94 us -> 36.1 us
    while x0 -> x32, local copies, waits for them, and re-layouts: none -> 31.3 us
    gather x0 -> x1, local copies, waits for them, and re-layouts: none -> 20.3 us  [ring_gather(): pieces = jnp.stack(pieces)[(mine - jnp.arange(peers)) % peers]]
    transpose x0 -> x1, local copies, waits for them, and re-layouts: none -> 19.5 us  [in_order(): return jnp.moveaxis(pieces, 0, dim).reshape(shape)]
    dynamic_slice x32 -> x48, local copies, waits for them, and re-layouts: 40 us -> 39.4 us  [select(): return lax.dynamic_slice_in_dim(source, col_start, HD, 1)]
  transfers between devices with their start and end apart: 4 -> 18, of which waited for: 3 -> 16; matrix products, arithmetic and copies ran while one was open for 38% -> 30% of each run, Pallas kernels for 0% -> 0%
where the time goes in v1:
time: 1030 us; the launch traced here: 1020 us
  waiting for transfers between devices  634 us (62%)
  local copies, waits for them, and re-layouts  169 us (16%)
  matrix products  151 us (15%)
  other arithmetic  39.2 us (4%)
  between operations  15.2 us (1%)
  loops' own time  10.8 us (1%)
    ppermute x15, waiting for transfers between devices, ring_gather(): pieces.append(lax.ppermute(pieces[-1], axis, upward))  632 us
    dot_general x16, matrix products, attend_whole(): jnp.dot(weights, value_rows, preferred_element_type=jnp.float32)  65 us
    dot_general x32, matrix products, score_block(): lax.dot_general(queries, key_rows, (((1,), (1,)), ((), ())), preferred_el...  57.3 us
    dynamic_slice x48, local copies, waits for them, and re-layouts, select(): return lax.dynamic_slice_in_dim(source, col_start, HD, 1)  39.4 us
    unnamed x49, local copies, waits for them, and re-layouts  36.1 us
    while x32, local copies, waits for them, and re-layouts  31.3 us
  transfers between devices with their start and end apart: 18, of which 16 were waited for; matrix products, arithmetic and copies ran while one was open for 30% of the time, Pallas kernels for 0%

profile of v1, /device:TPU:0, one launch (start us, length us, event | category | flops | bytes accessed | tf_op | source)
XLA Modules:
  0.0 1024.4 jit_solution(3991278282379765893)
XLA Ops:
  7.2 3.0 collective-permute-start
  10.2 42.8 %collective-permute-done = bf16[3,192,1536]{2,1,0:T(8,128)(2,1)S(1)} collective-permute-done((bf16[3,192,1536]{2,1,0:T(8,128)(2,1)}, bf16[3,192,1536]{2,1,0:T(8,128)(2,1)S(1)}, u32[]{:S(2)}, u32[]{:S(2)}) %collective-permute-start) | collective-permute-done | bytes 1769504 | tf_op jit(solution)/shard_map/ppermute | solution.py:24
  53.0 43.4 %collective-permute-done.1 = bf16[3,192,1536]{2,1,0:T(8,128)(2,1)S(1)} collective-permute-done((bf16[3,192,1536]{2,1,0:T(8,128)(2,1)S(1)}, bf16[3,192,1536]{2,1,0:T(8,128)(2,1)S(1)}, u32[]{:S(2)}, u32[]{:S(2)}) %collective-permute-start.1) | collective-permute-done | bytes 1769504 | tf_op jit(solution)/shard_map/ppermute | solution.py:24
  96.4 42.5 %collective-permute-done.2 = bf16[3,192,1536]{2,1,0:T(8,128)(2,1)S(1)} collective-permute-done((bf16[3,192,1536]{2,1,0:T(8,128)(2,1)S(1)}, bf16[3,192,1536]{2,1,0:T(8,128)(2,1)S(1)}, u32[]{:S(2)}, u32[]{:S(2)}) %collective-permute-start.2) | collective-permute-done | bytes 1769504 | tf_op jit(solution)/shard_map/ppermute | solution.py:24
  138.9 41.5 %collective-permute-done.3 = bf16[3,192,1536]{2,1,0:T(8,128)(2,1)S(1)} collective-permute-done((bf16[3,192,1536]{2,1,0:T(8,128)(2,1)S(1)}, bf16[3,192,1536]{2,1,0:T(8,128)(2,1)S(1)}, u32[]{:S(2)}, u32[]{:S(2)}) %collective-permute-start.3) | collective-permute-done | bytes 1769504 | tf_op jit(solution)/shard_map/ppermute | solution.py:24
  181.7 39.4 %collective-permute-done.4 = bf16[3,192,1536]{2,1,0:T(8,128)(2,1)S(1)} collective-permute-done((bf16[3,192,1536]{2,1,0:T(8,128)(2,1)S(1)}, bf16[3,192,1536]{2,1,0:T(8,128)(2,1)S(1)}, u32[]{:S(2)}, u32[]{:S(2)}) %collective-permute-start.4) | collective-permute-done | bytes 1769504 | tf_op jit(solution)/shard_map/ppermute | solution.py:24
  222.3 39.7 %collective-permute-done.5 = bf16[3,192,1536]{2,1,0:T(8,128)(2,1)S(1)} collective-permute-done((bf16[3,192,1536]{2,1,0:T(8,128)(2,1)S(1)}, bf16[3,192,1536]{2,1,0:T(8,128)(2,1)S(1)}, u32[]{:S(2)}, u32[]{:S(2)}) %collective-permute-start.5) | collective-permute-done | bytes 1769504 | tf_op jit(solution)/shard_map/ppermute | solution.py:24
  263.2 38.9 %collective-permute-done.6 = bf16[3,192,1536]{2,1,0:T(8,128)(2,1)} collective-permute-done((bf16[3,192,1536]{2,1,0:T(8,128)(2,1)S(1)}, bf16[3,192,1536]{2,1,0:T(8,128)(2,1)}, u32[]{:S(2)}, u32[]{:S(2)}) %collective-permute-start.6) | collective-permute-done | bytes 1769504 | tf_op jit(solution)/shard_map/ppermute | solution.py:24
  302.2 38.7 %collective-permute-done.7 = bf16[3,192,1536]{2,1,0:T(8,128)(2,1)} collective-permute-done((bf16[3,192,1536]{2,1,0:T(8,128)(2,1)}, bf16[3,192,1536]{2,1,0:T(8,128)(2,1)}, u32[]{:S(2)}, u32[]{:S(2)}) %collective-permute-start.7) | collective-permute-done | bytes 1769504 | tf_op jit(solution)/shard_map/ppermute | solution.py:24
  340.9 38.8 %collective-permute-done.8 = bf16[3,192,1536]{2,1,0:T(8,128)(2,1)} collective-permute-done((bf16[3,192,1536]{2,1,0:T(8,128)(2,1)}, bf16[3,192,1536]{2,1,0:T(8,128)(2,1)}, u32[]{:S(2)}, u32[]{:S(2)}) %collective-permute-start.8) | collective-permute-done | bytes 1769504 | tf_op jit(solution)/shard_map/ppermute | solution.py:24
  382.4 55.6 %collective-permute-done.9 = bf16[3,192,1536]{2,1,0:T(8,128)(2,1)} collective-permute-done((bf16[3,192,1536]{2,1,0:T(8,128)(2,1)}, bf16[3,192,1536]{2,1,0:T(8,128)(2,1)}, u32[]{:S(2)}, u32[]{:S(2)}) %collective-permute-start.9) | collective-permute-done | bytes 1769504 | tf_op jit(solution)/shard_map/ppermute | solution.py:24
  441.6 10.4 %slice_bitcast_fusion = (bf16[2048,1536]{1,0:T(8,128)(2,1)}, bf16[2048,1536]{1,0:T(8,128)(2,1)}) fusion(bf16[1,2,2048,1536]{3,2,1,0:T(8,128)(2,1)} %param.13), kind=kLoop, calls=%fused_computation.34 | loop fusion | bytes 25165824 | tf_op jit(solution)/shard_map/squeeze | solution.py:134
  452.0 56.8 %collective-permute-done.10 = bf16[3,192,1536]{2,1,0:T(8,128)(2,1)} collective-permute-done((bf16[3,192,1536]{2,1,0:T(8,128)(2,1)}, bf16[3,192,1536]{2,1,0:T(8,128)(2,1)}, u32[]{:S(2)}, u32[]{:S(2)}) %collective-permute-start.10) | collective-permute-done | bytes 1769504 | tf_op jit(solution)/shard_map/ppermute | solution.py:24
  510.6 2.6 fusion.21
  514.6 70.6 %collective-permute-done.11 = bf16[3,192,1536]{2,1,0:T(8,128)(2,1)} collective-permute-done((bf16[3,192,1536]{2,1,0:T(8,128)(2,1)}, bf16[3,192,1536]{2,1,0:T(8,128)(2,1)}, u32[]{:S(2)}, u32[]{:S(2)}) %collective-permute-start.11) | collective-permute-done | bytes 1769504 | tf_op jit(solution)/shard_map/ppermute | solution.py:24
  590.6 33.5 %collective-permute-done.12 = bf16[3,192,1536]{2,1,0:T(8,128)(2,1)S(1)} collective-permute-done((bf16[3,192,1536]{2,1,0:T(8,128)(2,1)}, bf16[3,192,1536]{2,1,0:T(8,128)(2,1)S(1)}, u32[]{:S(2)}, u32[]{:S(2)}) %collective-permute-start.12) | collective-permute-done | bytes 1769504 | tf_op jit(solution)/shard_map/ppermute | solution.py:24
  624.1 2.8 bitcast_dynamic-update-slice_fusion.8
  626.9 2.8 bitcast_dynamic-update-slice_fusion.7
  629.8 2.8 bitcast_dynamic-update-slice_fusion.6
  632.6 2.8 bitcast_dynamic-update-slice_fusion.5
  635.4 27.5 %collective-permute-done.13 = bf16[3,192,1536]{2,1,0:T(8,128)(2,1)S(1)} collective-permute-done((bf16[3,192,1536]{2,1,0:T(8,128)(2,1)S(1)}, bf16[3,192,1536]{2,1,0:T(8,128)(2,1)S(1)}, u32[]{:S(2)}, u32[]{:S(2)}) %collective-permute-start.13) | collective-permute-done | bytes 1769504 | tf_op jit(solution)/shard_map/ppermute | solution.py:24
  662.9 2.8 bitcast_dynamic-update-slice_fusion.4
  665.7 2.9 bitcast_dynamic-update-slice_fusion.3
  671.3 22.9 %collective-permute-done.14 = bf16[3,192,1536]{2,1,0:T(8,128)(2,1)S(1)} collective-permute-done((bf16[3,192,1536]{2,1,0:T(8,128)(2,1)S(1)}, bf16[3,192,1536]{2,1,0:T(8,128)(2,1)S(1)}, u32[]{:S(2)}, u32[]{:S(2)}) %collective-permute-start.14) | collective-permute-done | bytes 1769504 | tf_op jit(solution)/shard_map/ppermute | solution.py:24
  695.5 20.3 %gather_fusion = bf16[16,3,192,1536]{3,2,1,0:T(8,128)(2,1)} fusion(bf16[16,3,192,1536]{3,2,1,0:T(8,128)(2,1)} %bitcast_dynamic-update-slice_fusion, s32[1024]{0:T(1024)} %pad_clamp_fusion), kind=kCustom, calls=%fused_computation | custom fusion | bytes 56623168 | tf_op jit(solution)/shard_map/gather | solution.py:26
  715.9 19.5 %copy.28 = bf16[3,16,192,1536]{3,2,1,0:T(8,128)(2,1)} copy(bf16[3,16,192,1536]{3,2,0,1:T(8,128)(2,1)} %bitcast.75) | data formatting | bytes 56623104 | tf_op jit(solution)/shard_map/transpose | solution.py:16
  735.6 19.3 %convolution_bitcast_fusion = f32[3,512,1536]{1,2,0:T(8,128)S(1)} fusion(bf16[3,3072,1536]{2,1,0:T(8,128)(2,1)} %bitcast.76, bf16[512,3072]{1,0:T(8,128)(2,1)S(1)} %copy-done.1, f32[3072]{0:T(1024)S(1)} %bitcast.81, f32[512]{0:T(512)S(1)} %add_rsqrt_fusion), kind=kOutput, calls=%fused_computation.36 | convolution fusion | flops 14501806080 | bytes 40908800 | tf_op jit(solution)/shard_map/td,jdc->jtc/dot_general | solution.py:50
  758.4 2.3 broadcast_select_fusion
  760.7 237.8 %while.11 = (s32[]{:T(128)}, bf16[16,512,96]{1,2,0:T(8,128)(2,1)}, s32[]{:T(128)}, s32[16]{0:T(128)S(1)}, bf16[512,1536]{0,1:T(8,128)(2,1)}, /*index=5*/bf16[204...) while((s32[]{:T(128)}, bf16[16,512,96]{1,2,0:T(8,128)(2,1)}, ...), condition=%wide.region_5.6_spmd.clone, body=%wide.region_1.5_spmd.clone.sunk | while | flops 517981184 | bytes 35119856 | solution.py:99
  764.0 2.3 fusion.44
  771.6 4.1 fusion.46
  778.8 2.3 fusion.44
  786.5 4.1 fusion.46
  793.7 2.3 fusion.44
  801.3 4.1 fusion.46
  808.6 2.3 fusion.44
  816.2 4.1 fusion.46
  823.5 2.3 fusion.44
  831.1 4.1 fusion.46
  838.4 2.3 fusion.44
  846.0 4.1 fusion.46
  853.3 2.3 fusion.44
  860.9 4.1 fusion.46
  868.2 2.3 fusion.44
  875.8 4.1 fusion.46
  883.1 2.3 fusion.44
  890.7 4.1 fusion.46
  898.0 2.3 fusion.44
  905.6 4.1 fusion.46
  912.8 2.3 fusion.44
  920.4 4.1 fusion.46
  927.7 2.3 fusion.44
  935.3 4.1 fusion.46
  942.6 2.3 fusion.44
  950.2 4.1 fusion.46
  957.5 2.3 fusion.44
  965.1 4.1 fusion.46
  972.4 2.3 fusion.44
  980.0 4.1 fusion.46
  994.5 4.1 fusion.46
  998.6 9.5 convolution_convert_fusion
  1008.1 2.2 maximum_bitcast_fusion
  1010.3 2.8 copy.33
  1015.0 2.9 select_convert_fusion
  (241 shorter events, 154.9 us)
Async XLA Ops:
  7.2 373.9 %copy-start.2 = (bf16[3,192,1536]{2,1,0:T(8,128)(2,1)S(1)}, bf16[3,192,1536]{2,1,0:T(8,128)(2,1)}, u32[]{:S(2)}) copy-start(bf16[3,192,1536]{2,1,0:T(8,128)(2,1)} %param.11) | copy-start | bytes 5308420
  7.2 430.8 %copy-start.15 = (bf16[1536]{0:T(1024)(128)(2,1)S(1)}, bf16[1536]{0:T(1024)(128)(2,1)}, u32[]{:S(2)}) copy-start(bf16[1536]{0:T(1024)(128)(2,1)} %param.10) | copy-start | bytes 9220
  7.2 503.5 %all-gather.4.cloned.1.call-start = ((), (), s32[]{:S(2)}) async-start(), calls=%async_computation.1 | async-start | bytes 4718592 | tf_op jit(solution)/shard_map/all_gather | solution.py:105
  7.2 45.8 %collective-permute-start = (bf16[3,192,1536]{2,1,0:T(8,128)(2,1)}, bf16[3,192,1536]{2,1,0:T(8,128)(2,1)S(1)}, u32[]{:S(2)}, u32[]{:S(2)}) collective-permute-start(bf16[3,192,1536]{2,1,0:T(8,128)(2,1)} %param.11), channel_id=1, source_target_pairs={{0,2},{2,4},{4,6},{6,8},{8,10},{10,12},{12,14},{14,16},{16,18},{18... | collective-permute-start | bytes 5308424 | tf_op jit(solution)/shard_map/ppermute | solution.py:24
  53.0 43.4 %copy-start.7 = (bf16[3,192,1536]{2,1,0:T(8,128)(2,1)}, bf16[3,192,1536]{2,1,0:T(8,128)(2,1)S(1)}, u32[]{:S(2)}) copy-start(bf16[3,192,1536]{2,1,0:T(8,128)(2,1)S(1)} %collective-permute-done) | copy-start | bytes 5308420
  53.0 43.4 %collective-permute-start.1 = (bf16[3,192,1536]{2,1,0:T(8,128)(2,1)S(1)}, bf16[3,192,1536]{2,1,0:T(8,128)(2,1)S(1)}, u32[]{:S(2)}, u32[]{:S(2)}) collective-permute-start(bf16[3,192,1536]{2,1,0:T(8,128)(2,1)S(1)} %collective-permute-done), channel_id=1, source_target_pairs={{0,2},{2,4},{4,6},{6,8},{8,10},{10,12},{12,14},{14,16},{16,18},{18... | collective-permute-start | bytes 5308424 | tf_op jit(solution)/shard_map/ppermute | solution.py:24
  96.4 84.0 %copy-start.3 = (bf16[3,192,1536]{2,1,0:T(8,128)(2,1)}, bf16[3,192,1536]{2,1,0:T(8,128)(2,1)S(1)}, u32[]{:S(2)}) copy-start(bf16[3,192,1536]{2,1,0:T(8,128)(2,1)S(1)} %collective-permute-done.1) | copy-start | bytes 5308420
  96.4 42.5 %collective-permute-start.2 = (bf16[3,192,1536]{2,1,0:T(8,128)(2,1)S(1)}, bf16[3,192,1536]{2,1,0:T(8,128)(2,1)S(1)}, u32[]{:S(2)}, u32[]{:S(2)}) collective-permute-start(bf16[3,192,1536]{2,1,0:T(8,128)(2,1)S(1)} %collective-permute-done.1), channel_id=1, source_target_pairs={{0,2},{2,4},{4,6},{6,8},{8,10},{10,12},{12,14},{14,16},{16,18},{18... | collective-permute-start | bytes 5308424 | tf_op jit(solution)/shard_map/ppermute | solution.py:24
  138.9 41.5 %collective-permute-start.3 = (bf16[3,192,1536]{2,1,0:T(8,128)(2,1)S(1)}, bf16[3,192,1536]{2,1,0:T(8,128)(2,1)S(1)}, u32[]{:S(2)}, u32[]{:S(2)}) collective-permute-start(bf16[3,192,1536]{2,1,0:T(8,128)(2,1)S(1)} %collective-permute-done.2), channel_id=1, source_target_pairs={{0,2},{2,4},{4,6},{6,8},{8,10},{10,12},{12,14},{14,16},{16,18},{18... | collective-permute-start | bytes 5308424 | tf_op jit(solution)/shard_map/ppermute | solution.py:24
  180.4 1.2 copy-start.5
  180.4 40.6 %collective-permute-start.4 = (bf16[3,192,1536]{2,1,0:T(8,128)(2,1)S(1)}, bf16[3,192,1536]{2,1,0:T(8,128)(2,1)S(1)}, u32[]{:S(2)}, u32[]{:S(2)}) collective-permute-start(bf16[3,192,1536]{2,1,0:T(8,128)(2,1)S(1)} %collective-permute-done.3), channel_id=1, source_target_pairs={{0,2},{2,4},{4,6},{6,8},{8,10},{10,12},{12,14},{14,16},{16,18},{18... | collective-permute-start | bytes 5308424 | tf_op jit(solution)/shard_map/ppermute | solution.py:24
  221.1 1.3 copy-start.9
  222.3 39.7 %collective-permute-start.5 = (bf16[3,192,1536]{2,1,0:T(8,128)(2,1)S(1)}, bf16[3,192,1536]{2,1,0:T(8,128)(2,1)S(1)}, u32[]{:S(2)}, u32[]{:S(2)}) collective-permute-start(bf16[3,192,1536]{2,1,0:T(8,128)(2,1)S(1)} %collective-permute-done.4), channel_id=1, source_target_pairs={{0,2},{2,4},{4,6},{6,8},{8,10},{10,12},{12,14},{14,16},{16,18},{18... | collective-permute-start | bytes 5308424 | tf_op jit(solution)/shard_map/ppermute | solution.py:24
  262.0 1.2 copy-start.11
  263.2 38.9 %collective-permute-start.6 = (bf16[3,192,1536]{2,1,0:T(8,128)(2,1)S(1)}, bf16[3,192,1536]{2,1,0:T(8,128)(2,1)}, u32[]{:S(2)}, u32[]{:S(2)}) collective-permute-start(bf16[3,192,1536]{2,1,0:T(8,128)(2,1)S(1)} %collective-permute-done.5), channel_id=1, source_target_pairs={{0,2},{2,4},{4,6},{6,8},{8,10},{10,12},{12,14},{14,16},{16,18},{18... | collective-permute-start | bytes 5308424 | tf_op jit(solution)/shard_map/ppermute | solution.py:24
  302.1 38.8 %collective-permute-start.7 = (bf16[3,192,1536]{2,1,0:T(8,128)(2,1)}, bf16[3,192,1536]{2,1,0:T(8,128)(2,1)}, u32[]{:S(2)}, u32[]{:S(2)}) collective-permute-start(bf16[3,192,1536]{2,1,0:T(8,128)(2,1)} %collective-permute-done.6), channel_id=1, source_target_pairs={{0,2},{2,4},{4,6},{6,8},{8,10},{10,12},{12,14},{14,16},{16,18},{18... | collective-permute-start | bytes 5308424 | tf_op jit(solution)/shard_map/ppermute | solution.py:24
  302.2 696.4 %all-gather.6.cloned.1.call-start = ((), (), s32[]{:S(2)}) async-start(), calls=%async_computation.2 | async-start | bytes 10027008 | tf_op jit(solution)/shard_map/all_gather | solution.py:141
  340.9 38.8 %collective-permute-start.8 = (bf16[3,192,1536]{2,1,0:T(8,128)(2,1)}, bf16[3,192,1536]{2,1,0:T(8,128)(2,1)}, u32[]{:S(2)}, u32[]{:S(2)}) collective-permute-start(bf16[3,192,1536]{2,1,0:T(8,128)(2,1)} %collective-permute-done.7), channel_id=1, source_target_pairs={{0,2},{2,4},{4,6},{6,8},{8,10},{10,12},{12,14},{14,16},{16,18},{18... | collective-permute-start | bytes 5308424 | tf_op jit(solution)/shard_map/ppermute | solution.py:24
  379.7 58.3 %collective-permute-start.9 = (bf16[3,192,1536]{2,1,0:T(8,128)(2,1)}, bf16[3,192,1536]{2,1,0:T(8,128)(2,1)}, u32[]{:S(2)}, u32[]{:S(2)}) collective-permute-start(bf16[3,192,1536]{2,1,0:T(8,128)(2,1)} %collective-permute-done.8), channel_id=1, source_target_pairs={{0,2},{2,4},{4,6},{6,8},{8,10},{10,12},{12,14},{14,16},{16,18},{18... | collective-permute-start | bytes 5308424 | tf_op jit(solution)/shard_map/ppermute | solution.py:24
  379.7 635.3 %reduce-scatter.2.cloned.1.call-start = ((), (), s32[]{:S(2)}) async-start(), calls=%async_computation.3 | async-start | bytes 4718592 | tf_op jit(solution)/shard_map/reduce_scatter | solution.py:144
  438.0 70.8 %collective-permute-start.10 = (bf16[3,192,1536]{2,1,0:T(8,128)(2,1)}, bf16[3,192,1536]{2,1,0:T(8,128)(2,1)}, u32[]{:S(2)}, u32[]{:S(2)}) collective-permute-start(bf16[3,192,1536]{2,1,0:T(8,128)(2,1)} %collective-permute-done.9), channel_id=1, source_target_pairs={{0,2},{2,4},{4,6},{6,8},{8,10},{10,12},{12,14},{14,16},{16,18},{18... | collective-permute-start | bytes 5308424 | tf_op jit(solution)/shard_map/ppermute | solution.py:24
  441.6 67.7 %copy-start.8 = (bf16[3,192,1536]{2,1,0:T(8,128)(2,1)S(1)}, bf16[3,192,1536]{2,1,0:T(8,128)(2,1)}, u32[]{:S(2)}) copy-start(bf16[3,192,1536]{2,1,0:T(8,128)(2,1)} %copy-done.7) | copy-start | bytes 5308420
  508.8 76.4 %collective-permute-start.11 = (bf16[3,192,1536]{2,1,0:T(8,128)(2,1)}, bf16[3,192,1536]{2,1,0:T(8,128)(2,1)}, u32[]{:S(2)}, u32[]{:S(2)}) collective-permute-start(bf16[3,192,1536]{2,1,0:T(8,128)(2,1)} %collective-permute-done.10), channel_id=1, source_target_pairs={{0,2},{2,4},{4,6},{6,8},{8,10},{10,12},{12,14},{14,16},{16,18},{18... | collective-permute-start | bytes 5308424 | tf_op jit(solution)/shard_map/ppermute | solution.py:24
  509.3 3.9 copy-start.4
  513.2 73.3 %copy-start.6 = (bf16[3,192,1536]{2,1,0:T(8,128)(2,1)S(1)}, bf16[3,192,1536]{2,1,0:T(8,128)(2,1)}, u32[]{:S(2)}) copy-start(bf16[3,192,1536]{2,1,0:T(8,128)(2,1)} %copy-done.5) | copy-start | bytes 5308420
  514.6 73.3 %copy-start.10 = (bf16[3,192,1536]{2,1,0:T(8,128)(2,1)S(1)}, bf16[3,192,1536]{2,1,0:T(8,128)(2,1)}, u32[]{:S(2)}) copy-start(bf16[3,192,1536]{2,1,0:T(8,128)(2,1)} %copy-done.9) | copy-start | bytes 5308420
  585.2 39.0 %collective-permute-start.12 = (bf16[3,192,1536]{2,1,0:T(8,128)(2,1)}, bf16[3,192,1536]{2,1,0:T(8,128)(2,1)S(1)}, u32[]{:S(2)}, u32[]{:S(2)}) collective-permute-start(bf16[3,192,1536]{2,1,0:T(8,128)(2,1)} %collective-permute-done.11), channel_id=1, source_target_pairs={{0,2},{2,4},{4,6},{6,8},{8,10},{10,12},{12,14},{14,16},{16,18},{18... | collective-permute-start | bytes 5308424 | tf_op jit(solution)/shard_map/ppermute | solution.py:24
  586.5 2.7 copy-start.12
  624.1 38.8 %collective-permute-start.13 = (bf16[3,192,1536]{2,1,0:T(8,128)(2,1)S(1)}, bf16[3,192,1536]{2,1,0:T(8,128)(2,1)S(1)}, u32[]{:S(2)}, u32[]{:S(2)}) collective-permute-start(bf16[3,192,1536]{2,1,0:T(8,128)(2,1)S(1)} %collective-permute-done.12), channel_id=1, source_target_pairs={{0,2},{2,4},{4,6},{6,8},{8,10},{10,12},{12,14},{14,16},{16,18},{18... | collective-permute-start | bytes 5308424 | tf_op jit(solution)/shard_map/ppermute | solution.py:24
  662.9 31.3 %collective-permute-start.14 = (bf16[3,192,1536]{2,1,0:T(8,128)(2,1)S(1)}, bf16[3,192,1536]{2,1,0:T(8,128)(2,1)S(1)}, u32[]{:S(2)}, u32[]{:S(2)}) collective-permute-start(bf16[3,192,1536]{2,1,0:T(8,128)(2,1)S(1)} %collective-permute-done.13), channel_id=1, source_target_pairs={{0,2},{2,4},{4,6},{6,8},{8,10},{10,12},{12,14},{14,16},{16,18},{18... | collective-permute-start | bytes 5308424 | tf_op jit(solution)/shard_map/ppermute | solution.py:24
  715.9 19.8 %copy-start.1 = (bf16[512,3072]{1,0:T(8,128)(2,1)S(1)}, bf16[512,3072]{1,0:T(8,128)(2,1)}, u32[]{:S(2)}) copy-start(bf16[512,3072]{1,0:T(8,128)(2,1)} %all-gather.4.cloned.1.call-done) | copy-start | bytes 9437188
  754.9 0.9 copy-start.13
  754.9 0.9 copy-start.14
  757.0 1.4 copy-start.16
  766.2 2.0 copy-start
  781.1 2.0 copy-start
  796.0 2.0 copy-start
  810.9 2.0 copy-start
  825.8 2.0 copy-start
  840.7 2.0 copy-start
  855.6 2.0 copy-start
  870.5 2.0 copy-start
  885.4 2.0 copy-start
  900.2 2.0 copy-start
  915.1 2.0 copy-start
  930.0 2.0 copy-start
  944.9 2.0 copy-start
  959.8 2.0 copy-start
  974.7 2.0 copy-start
  989.4 2.0 copy-start
Sparse Core Ops, SparseCore 0:
  302.3 13.4 all-gather.3
  379.8 187.0 all-gather.5
  1008.2 6.7 reduce-scatter.1
